TPU v7x, 512 devices: a whole 4x8x8 slice. The times are simulated.
512 devices in a mesh: expert: 128 (over y, z, core), dp: 4 (over x).
Axes of the slice: x: 4, y: 8, z: 8, core: 2. Of those that a mesh axis runs over, the one named last changes fastest.
Arguments:
- hidden: bfloat16 [128, 4, 256, 1024], P('expert', 'dp'), may hold values from -6 to 6
- w_down: bfloat16 [128, 1024, 3584], P('expert', 'dp'), may hold values from -0.1875 to 0.1875
- expert_ids: int32 [4, 2048, 8], P('dp', 'expert'), may hold values from 0 to 127, all different within a row; in each aligned block of 16 rows (0 to 15, 16 to 31, ..., all dimensions but the last counted through in order) at most 2 rows name the same one
- route_weights: float32 [4, 2048, 8], P('dp', 'expert'), may hold values from 0.1 to 0.6
- grad_out: bfloat16 [4, 2048, 3584], P('dp', 'expert'), may hold values from -6 to 6
Outputs:
- mixed: bfloat16 [4, 2048, 3584], P('dp', 'expert')
- d_hidden: bfloat16 [128, 4, 256, 1024], P('expert', 'dp')
- d_w_down: bfloat16 [128, 1024, 3584], P('expert', 'dp')
- d_route: float32 [4, 2048, 8], P('dp', 'expert')
Inputs may be any that keep to these rules, and one draw needn't show every extreme that they name: `expert_ids`: among the 16 tokens of one device no expert is chosen more than 2 times, and some expert is chosen exactly 2 times; the 8 choices of a token are distinct.
All inputs are finite; a program needn't handle non-finite values.
Results may differ from a plain program's by a relative error of at most 0.0085.
Values may be sent and summed in bfloat16 or wider, within the bound.
A program may use at most 128 MiB of HBM per device.

v0:
```python
import jax
import jax.numpy as jnp
from jax import lax
from jax.sharding import PartitionSpec as P


def slot_ranks(choices, experts):
    flat = choices.reshape(-1)
    onehot = (flat[:, None] == jnp.arange(experts, dtype=jnp.int32)[None, :]).astype(jnp.int32)
    earlier = jnp.cumsum(onehot, axis=0) - onehot
    return jnp.sum(earlier * onehot, axis=1).reshape(choices.shape)


def on_device(hidden, w_down, expert_ids, route_weights, grad_out):
    experts = lax.axis_size("expert")
    groups = lax.axis_size("dp")
    slots = hidden.shape[2] // experts
    width = w_down.shape[2]
    w_whole = lax.all_gather(w_down, "dp", axis=1, tiled=True)[0]
    out_slots = jnp.dot(hidden[0, 0], w_whole, preferred_element_type=jnp.float32).astype(
        jnp.bfloat16
    )
    arrived = lax.all_to_all(
        out_slots.reshape(experts, slots, width), "expert", split_axis=0, concat_axis=0, tiled=True
    )
    arrived = arrived.reshape(experts * slots, width)
    choices = expert_ids[0]
    weights = route_weights[0]
    cotangent = grad_out[0].astype(jnp.float32)
    rows = choices * slots + slot_ranks(choices, experts)
    out_pair = arrived[rows].astype(jnp.float32)
    mixed = jnp.einsum("tk,tkd->td", weights, out_pair)
    d_route = jnp.einsum("td,tkd->tk", cotangent, out_pair)
    grad_pair = (weights[..., None] * cotangent[:, None, :]).astype(jnp.bfloat16)
    outgoing = jnp.zeros((experts * slots, width), jnp.bfloat16)
    outgoing = outgoing.at[rows.reshape(-1)].set(grad_pair.reshape(-1, width))
    mine = lax.all_to_all(
        outgoing.reshape(experts, 1, slots, width),
        "expert",
        split_axis=0,
        concat_axis=0,
        tiled=True,
    )
    own_grads = mine[:, 0]
    d_hidden = jnp.einsum(
        "rd,hd->rh", own_grads.reshape(-1, width), w_whole, preferred_element_type=jnp.float32
    ).astype(jnp.bfloat16)
    columns = lax.all_to_all(hidden, "dp", split_axis=3, concat_axis=1, tiled=True)[0]
    columns = columns.reshape(groups, experts, slots, columns.shape[-1])
    cw = width // 2
    parts = []
    for c in range(2):
        slot_grads = lax.all_gather(mine[..., c * cw : (c + 1) * cw], "dp", axis=1, tiled=True)
        parts.append(
            jnp.einsum(
                "gsch,sgcd->hd", columns, slot_grads, preferred_element_type=jnp.float32
            ).astype(jnp.bfloat16)
        )
    d_weight = jnp.concatenate(parts, axis=1)
    return (
        mixed.astype(jnp.bfloat16)[None],
        d_hidden.reshape(hidden.shape),
        d_weight[None],
        d_route[None],
    )


def solution(mesh):
    placed = (
        P("expert", "dp", None, None),
        P("expert", "dp", None),
        P("dp", "expert", None),
        P("dp", "expert", None),
        P("dp", "expert", None),
    )
    return jax.shard_map(
        on_device,
        mesh=mesh,
        in_specs=placed,
        out_specs=(
            P("dp", "expert", None),
            P("expert", "dp", None, None),
            P("expert", "dp", None),
            P("dp", "expert", None),
        ),
        check_vma=False,
    )
```

profile of v0, /device:TPU:1, one launch (start us, length us, event | category | flops | bytes accessed | tf_op | source)
XLA Modules:
  0.0 227.6 jit_solution(7683013739206800182)
XLA Ops:
  7.2 0.7 all-gather.4.cloned.1.call-update
  9.0 2.5 %scatter_custom_fusion = bf16[256,3584]{1,0:T(8,128)(2,1)S(1)} fusion(s32[128]{0:T(128)S(1)} %fusion.33, f32[16,3584]{1,0:T(8,128)S(1)} %bitcast_convert_fusion.1, f32[128]{0:T(128)S(1)} %mul.53, bf16[]{:T(256)} %constant.7.clone.1), kind=kCustom, calls=%fused_computation.18 | custom fusion | flops 917504 | bytes 2064898 | tf_op jit(solution)/shard_map/scatter | solution.py:36
  11.5 1.6 reshape.99
  13.2 64.9 %all_to_all.25 = bf16[128,1,2,3584]{3,2,1,0:T(2,128)(2,1)S(1)} all-to-all(bf16[128,1,2,3584]{3,2,1,0:T(2,128)(2,1)} %bitcast.87), channel_id=1, replica_groups=mesh['expert'=128,'dp'=4] {'expert'}, dimensions={0} | all-to-all | bytes 3670016 | tf_op jit(solution)/shard_map/all_to_all | solution.py:37
  78.1 2.2 fusion.34
  80.2 3.6 %copy.71 = bf16[128,1,2,1792]{0,3,1,2:T(8,128)(2,1)} copy(bf16[128,1,2,1792]{3,2,1,0:T(2,128)(2,1)} %get-tuple-element.24) | data formatting | bytes 1835008
  83.9 2.1 copy.72
  86.0 0.9 copy.58
  87.4 3.8 %reduce = bf16[1024,256]{1,0:T(8,128)(2,1)S(1)} reduce(bf16[1024,1,1,256]{3,2,1,0:T(2,128)(2,1)S(1)} %bitcast.89, bf16[]{:T(256)} %broadcast.58), dimensions={1,2}, to_apply=%bitcast.78.reduce_sub_computation | reduce | bytes 1048578
  91.3 0.9 reshape.126
  92.2 4.0 %all-to-all-start.2 = ((bf16[4,2,32768]{2,1,0:T(2,128)(2,1)}), bf16[4,2,32768]{2,1,0:T(2,128)(2,1)S(1)}, u32[]{:S(2)}, u32[]{:S(2)}) async-start(bf16[4,2,32768]{2,1,0:T(2,128)(2,1)} %reshape.126), calls=%async_computation.2 | async-start | bytes 1048576 | tf_op jit(solution)/shard_map/all_to_all | solution.py:48
  96.2 6.4 %fusion.4 = bf16[256,3584]{1,0:T(8,128)(2,1)} fusion(bf16[1,1024,3584]{2,1,0:T(8,128)(2,1)} %all-gather.4.cloned.1.call-done, bf16[1,1,256,1024]{3,2,1,0:T(8,128)(2,1)S(1)} %copy-done.1), kind=kOutput, calls=%fused_computation.6 | convolution fusion | flops 1879965696 | bytes 9699328 | tf_op jit(solution)/shard_map/dot_general | solution.py:20
  102.6 4.8 %reshape.96 = bf16[128,2,3584]{2,1,0:T(2,128)(2,1)} reshape(bf16[256,3584]{1,0:T(8,128)(2,1)} %fusion.4) | data formatting | bytes 3670016 | tf_op jit(solution)/shard_map/reshape | solution.py:24
  107.3 15.9 %all-to-all-start = ((bf16[128,2,3584]{2,1,0:T(2,128)(2,1)}), bf16[128,2,3584]{2,1,0:T(2,128)(2,1)}, u32[]{:S(2)}, u32[]{:S(2)}) async-start(bf16[128,2,3584]{2,1,0:T(2,128)(2,1)} %reshape.96), calls=%async_computation | async-start | bytes 3670016 | tf_op jit(solution)/shard_map/all_to_all | solution.py:23
  124.3 1.1 copy.59
  125.3 1.7 reshape_squeeze.6
  127.0 22.5 %all-gather.6.cloned.1.call-done = bf16[128,4,2,1792]{0,3,1,2:T(8,128)(2,1)} async-done(((bf16[128,1,2,1792]{0,3,1,2:T(8,128)(2,1)}), bf16[128,4,2,1792]{0,3,1,2:T(8,128)(2,1)}) %all-gather.6.cloned.1.call-update) | async-done | bytes 3670032 | tf_op jit(solution)/shard_map/all_gather | solution.py:53
  149.5 3.2 %fusion.10 = bf16[256,1792]{0,1:T(8,128)(2,1)S(1)} fusion(bf16[128,4,2,1792]{0,3,1,2:T(8,128)(2,1)} %all-gather.6.cloned.1.call-done, bf16[4,128,2,256]{3,0,2,1:T(4,128)(2,1)S(1)} %bitcast.91), kind=kOutput, calls=%fused_computation.12 | convolution fusion | flops 939982848 | bytes 5111808 | tf_op jit(solution)/shard_map/gsch,sgcd->hd/dot_general | solution.py:55
  152.7 48.4 %all-gather.8.cloned.1.call-done = bf16[128,4,2,1792]{0,3,1,2:T(8,128)(2,1)} async-done(((bf16[128,1,2,1792]{0,3,1,2:T(8,128)(2,1)}), bf16[128,4,2,1792]{0,3,1,2:T(8,128)(2,1)}) %all-gather.8.cloned.1.call-update) | async-done | bytes 3670032 | tf_op jit(solution)/shard_map/all_gather | solution.py:53
  201.1 3.2 %fusion.9 = bf16[256,1792]{0,1:T(8,128)(2,1)S(1)} fusion(bf16[128,4,2,1792]{0,3,1,2:T(8,128)(2,1)} %all-gather.8.cloned.1.call-done, bf16[4,128,2,256]{3,0,2,1:T(4,128)(2,1)S(1)} %bitcast.92), kind=kOutput, calls=%fused_computation.11 | convolution fusion | flops 939982848 | bytes 5111808 | tf_op jit(solution)/shard_map/gsch,sgcd->hd/dot_general | solution.py:55
  204.4 2.6 %copy.63 = bf16[1,256,3584]{2,1,0:T(8,128)(2,1)} copy(bf16[1,256,3584]{1,2,0:T(8,128)(2,1)S(1)} %maximum_bitcast_fusion) | data formatting | bytes 3670016
  207.0 6.5 %fusion.15 = bf16[1,1,256,1024]{3,2,1,0:T(8,128)(2,1)} fusion(bf16[256,3584]{1,0:T(8,128)(2,1)} %reshape_squeeze.6, bf16[1,1024,3584]{2,1,0:T(8,128)(2,1)} %all-gather.4.cloned.1.call-done), kind=kOutput, calls=%fused_computation.17 | convolution fusion | flops 1879310336 | bytes 9699328 | tf_op jit(solution)/shard_map/rd,hd->rh/dot_general | solution.py:45
  213.5 4.1 %reshape.97 = bf16[256,3584]{1,0:T(8,128)(2,1)S(1)} reshape(bf16[128,2,3584]{2,1,0:T(2,128)(2,1)} %all-to-all-done) | data formatting | bytes 3670016 | tf_op jit(solution)/shard_map/reshape | solution.py:26
  217.6 1.1 gather_fusion
  (47 shorter events, 5.1 us)
Async XLA Ops:
  7.2 0.8 copy-start.4
  7.2 1.1 copy-start.5
  7.2 1.8 copy-start.3
  7.2 89.0 %all-gather.4.cloned.1.call-start = ((), (), s32[]{:S(2)}) async-start(), calls=%async_computation.3 | async-start | bytes 9175040 | tf_op jit(solution)/shard_map/all_gather | solution.py:19
  7.9 141.6 %all-gather.6.cloned.1.call-start = ((), (), s32[]{:S(2)}) async-start(), calls=%async_computation.4 | async-start | bytes 4587520 | tf_op jit(solution)/shard_map/all_gather | solution.py:53
  83.8 2.2 copy-start
  83.8 117.3 %all-gather.8.cloned.1.call-start = ((), (), s32[]{:S(2)}) async-start(), calls=%async_computation.5 | async-start | bytes 4587520 | tf_op jit(solution)/shard_map/all_gather | solution.py:53
  91.3 4.9 %copy-start.1 = (bf16[1,1,256,1024]{3,2,1,0:T(8,128)(2,1)S(1)}, bf16[1,1,256,1024]{3,2,1,0:T(8,128)(2,1)}, u32[]{:S(2)}) copy-start(bf16[1,1,256,1024]{3,2,1,0:T(8,128)(2,1)} %param.5) | copy-start | bytes 1572868
  92.2 15.2 %all-to-all-start.2 = ((bf16[4,2,32768]{2,1,0:T(2,128)(2,1)}), bf16[4,2,32768]{2,1,0:T(2,128)(2,1)S(1)}, u32[]{:S(2)}, u32[]{:S(2)}) async-start(bf16[4,2,32768]{2,1,0:T(2,128)(2,1)} %reshape.126), calls=%async_computation.2 | async-start | bytes 1048576 | tf_op jit(solution)/shard_map/all_to_all | solution.py:48
  107.3 106.2 %all-to-all-start = ((bf16[128,2,3584]{2,1,0:T(2,128)(2,1)}), bf16[128,2,3584]{2,1,0:T(2,128)(2,1)}, u32[]{:S(2)}, u32[]{:S(2)}) async-start(bf16[128,2,3584]{2,1,0:T(2,128)(2,1)} %reshape.96), calls=%async_computation | async-start | bytes 3670016 | tf_op jit(solution)/shard_map/all_to_all | solution.py:23
  125.3 24.2 %copy-start.2 = (bf16[1,4,1,256,256]{4,1,3,2,0:T(4,128)(2,1)S(1)}, bf16[1,4,1,256,256]{4,1,3,2,0:T(4,128)(2,1)}, u32[]{:S(2)}) copy-start(bf16[1,4,1,256,256]{4,1,3,2,0:T(4,128)(2,1)} %copy.59) | copy-start | bytes 1572868
Sparse Core Ops, SparseCore 0:
  10.1 84.9 all-gather.3
  97.2 52.2 all-gather.5
  151.6 49.4 all-gather.7
where the time goes:
time: 228 us
  waiting for transfers between devices  71.7 us (31%)
  blocking collectives  64.9 us (28%)
  local copies, waits for them, and re-layouts  29.9 us (13%)
  matrix products  20.3 us (9%)
  starting transfers between devices  20 us (9%)
  between operations  14 us (6%)
  other arithmetic  6.95 us (3%)
    all_gather x2, waiting for transfers between devices, on_device(): lax.all_gather(mine[..., c * cw:(c + 1) * cw], 'dp', axis=1, tiled=True)  70.9 us
    all_to_all x1, blocking collectives, on_device(): lax.all_to_all(outgoing.reshape(experts, 1, slots, width), 'expert', spli...  64.9 us
    all_to_all x1, starting transfers between devices, on_device(): lax.all_to_all(out_slots.reshape(experts, slots, width), 'expert', split_...  15.9 us
    unnamed x22, local copies, waits for them, and re-layouts  11.3 us
    dot_general x1, matrix products, on_device(): jnp.einsum('rd,hd->rh', own_grads.reshape(-1, width), w_whole, preferred_...  6.53 us
    dot_general x1, matrix products, on_device(): jnp.dot(hidden[0, 0], w_whole, preferred_element_type=jnp.float32)  6.37 us
    dot_general x2, matrix products, on_device(): jnp.einsum('gsch,sgcd->hd', columns, slot_grads, preferred_element_type=j...  6.36 us
    reshape x1, local copies, waits for them, and re-layouts, on_device(): out_slots.reshape(experts, slots, width)  4.77 us
  transfers between devices with their start and end apart: 5, of which 2 were waited for; matrix products, arithmetic and copies ran while one was open for 22% of the time, Pallas kernels for 0%

commit v1 on v0

--- a/solution.py
+++ b/solution.py
@@ -1,7 +1,20 @@
+import functools
 import jax
 import jax.numpy as jnp
 from jax import lax
 from jax.sharding import PartitionSpec as P
+
+
+def recover_sample_for(arr, dim_no):
+    samples = []
+    for _ in range(lax.axis_size("dp")):
+        samples.append(arr)
+    response = jnp.stack(samples, axis=0)
+    carry_out = lax.all_to_all(response, "dp", 0, 0)
+    return jnp.concatenate(carry_out, axis=dim_no)
+
+
+strips_all_recover = functools.partial(recover_sample_for, dim_no=1)
 
 
 def slot_ranks(choices, experts):
@@ -50,7 +63,7 @@
     cw = width // 2
     parts = []
     for c in range(2):
-        slot_grads = lax.all_gather(mine[..., c * cw : (c + 1) * cw], "dp", axis=1, tiled=True)
+        slot_grads = strips_all_recover(mine[..., c * cw : (c + 1) * cw])
         parts.append(
             jnp.einsum(
                 "gsch,sgcd->hd", columns, slot_grads, preferred_element_type=jnp.float32

time: 228 us -> 270 us (1.18)
  waiting for transfers between devices: 71.7 us -> 145 us
  blocking collectives: 64.9 us -> 0 us
  starting transfers between devices: 20 us -> 46.6 us
  local copies, waits for them, and re-layouts: 29.9 us -> 36.1 us
    all_to_all x0 -> x3, waiting for transfers between devices: none -> 108 us  [the longest x2 67.4 us: recover_sample_for(): carry_out = lax.all_to_all(response, 'dp', 0, 0)]
    all_gather x2 -> x0, waiting for transfers between devices: 70.9 us -> none  [on_device(): lax.all_gather(mine[..., c * cw:(c + 1) * cw], 'dp', axis=1, tiled=True)]
    all_to_all x1 -> x0, blocking collectives: 64.9 us -> none  [on_device(): lax.all_to_all(outgoing.reshape(experts, 1, slots, width), 'expert', spli...]
    all_to_all x0 -> x3, starting transfers between devices: none -> 28.3 us  [the longest x1 18.5 us: on_device(): lax.all_to_all(outgoing.reshape(experts, 1, slots, width), 'expert', spli...]
    all_to_all x1, waiting for transfers between devices: 0.01 us -> 27.6 us  [on_device(): lax.all_to_all(out_slots.reshape(experts, slots, width), 'expert', split_...]
    all_to_all x1, waiting for transfers between devices: 0.01 us -> 9.34 us  [on_device(): lax.all_to_all(hidden, 'dp', split_axis=3, concat_axis=1, tiled=True)[0]]
    another operation x0 -> x2, local copies, waits for them, and re-layouts: none -> 6.98 us  [recover_sample_for(): response = jnp.stack(samples, axis=0)]
    slice x1 -> x3, local copies, waits for them, and re-layouts: 2.18 us -> 7.9 us  [on_device(): slot_grads = strips_all_recover(mine[..., c * cw:(c + 1) * cw])]
  transfers between devices with their start and end apart: 5 -> 6, of which waited for: 2 -> 5; matrix products, arithmetic and copies ran while one was open for 22% -> 21% of each run, Pallas kernels for 0% -> 0%
where the time goes in v1:
time: 270 us
  waiting for transfers between devices  145 us (54%)
  starting transfers between devices  46.6 us (17%)
  local copies, waits for them, and re-layouts  36.1 us (13%)
  matrix products  20.3 us (8%)
  between operations  14.3 us (5%)
  other arithmetic  6.96 us (3%)
    all_to_all x2, waiting for transfers between devices, recover_sample_for(): carry_out = lax.all_to_all(response, 'dp', 0, 0)  67.4 us
    all_to_all x1, waiting for transfers between devices, on_device(): lax.all_to_all(outgoing.reshape(experts, 1, slots, width), 'expert', spli...  40.3 us
    all_to_all x1, waiting for transfers between devices, on_device(): lax.all_to_all(out_slots.reshape(experts, slots, width), 'expert', split_...  27.6 us
    all_to_all x1, starting transfers between devices, on_device(): lax.all_to_all(outgoing.reshape(experts, 1, slots, width), 'expert', spli...  18.5 us
    all_to_all x1, starting transfers between devices, on_device(): lax.all_to_all(out_slots.reshape(experts, slots, width), 'expert', split_...  14.3 us
    all_to_all x2, starting transfers between devices, recover_sample_for(): carry_out = lax.all_to_all(response, 'dp', 0, 0)  9.81 us
    all_to_all x1, waiting for transfers between devices, on_device(): lax.all_to_all(hidden, 'dp', split_axis=3, concat_axis=1, tiled=True)[0]  9.34 us
    slice x3, local copies, waits for them, and re-layouts, on_device(): slot_grads = strips_all_recover(mine[..., c * cw:(c + 1) * cw])  7.9 us
  transfers between devices with their start and end apart: 6, of which 5 were waited for; matrix products, arithmetic and copies ran while one was open for 21% of the time, Pallas kernels for 0%

profile of v1, /device:TPU:1, one launch (start us, length us, event | category | flops | bytes accessed | tf_op | source)
XLA Modules:
  0.0 269.6 jit_solution(16284196985000452039)
XLA Ops:
  8.9 2.5 scatter_custom_fusion
  13.1 18.5 %all-to-all-start.1 = ((bf16[128,1,2,3584]{3,2,1,0:T(2,128)(2,1)}), bf16[128,1,2,3584]{3,2,1,0:T(2,128)(2,1)S(1)}, u32[]{:S(2)}, u32[]{:S(2)}) async-start(bf16[128,1,2,3584]{3,2,1,0:T(2,128)(2,1)} %bitcast.111), calls=%async_computation.1 | async-start | bytes 3670016 | tf_op jit(solution)/shard_map/all_to_all | solution.py:50
  33.1 3.8 %reduce = bf16[1024,256]{1,0:T(8,128)(2,1)S(1)} reduce(bf16[1024,1,1,256]{3,2,1,0:T(2,128)(2,1)S(1)} %bitcast.113, bf16[]{:T(256)} %broadcast.64), dimensions={1,2}, to_apply=%bitcast.104.reduce_sub_computation | reduce | bytes 1048578
  37.8 40.3 %all-to-all-done.1 = bf16[128,1,2,3584]{3,2,1,0:T(2,128)(2,1)S(1)} async-done(((bf16[128,1,2,3584]{3,2,1,0:T(2,128)(2,1)}), bf16[128,1,2,3584]{3,2,1,0:T(2,128)(2,1)S(1)}, u32[]{:S(2)}, u32[]{:S(2)}) %all-to-all-start.1) | async-done | bytes 1835040 | tf_op jit(solution)/shard_map/all_to_all | solution.py:50
  78.1 4.0 %all-to-all-start.3 = ((bf16[4,2,32768]{2,1,0:T(2,128)(2,1)}), bf16[4,2,32768]{2,1,0:T(2,128)(2,1)S(1)}, u32[]{:S(2)}, u32[]{:S(2)}) async-start(bf16[4,2,32768]{2,1,0:T(2,128)(2,1)} %reshape.148), calls=%async_computation.3 | async-start | bytes 1048576 | tf_op jit(solution)/shard_map/all_to_all | solution.py:61
  82.2 2.2 slice_bitcast_fusion.1
  84.3 3.6 %copy.51 = bf16[128,2,1792]{0,2,1:T(8,128)(2,1)} copy(bf16[128,2,1792]{2,1,0:T(2,128)(2,1)} %get-tuple-element.21) | data formatting | bytes 1835008 | tf_op jit(solution)/shard_map/slice | solution.py:66
  87.9 9.3 %all-to-all-done.3 = bf16[4,2,32768]{2,1,0:T(2,128)(2,1)S(1)} async-done(((bf16[4,2,32768]{2,1,0:T(2,128)(2,1)}), bf16[4,2,32768]{2,1,0:T(2,128)(2,1)S(1)}, u32[]{:S(2)}, u32[]{:S(2)}) %all-to-all-start.3) | async-done | bytes 524320 | tf_op jit(solution)/shard_map/all_to_all | solution.py:61
  97.3 3.5 %stack.5 = bf16[4,128,1,2,1792]{1,4,3,2,0:T(8,128)(2,1)} broadcast(bf16[128,2,1792]{0,2,1:T(8,128)(2,1)} %copy.51), dimensions={1,3,4} | broadcast | bytes 4587520 | tf_op jit(solution)/shard_map/stack | solution.py:12
  100.8 4.9 %all-to-all-start.4 = ((bf16[4,128,1,2,1792]{1,4,3,2,0:T(8,128)(2,1)}), bf16[4,128,1,2,1792]{1,4,3,2,0:T(8,128)(2,1)}, u32[]{:S(2)}, u32[]{:S(2)}) async-start(bf16[4,128,1,2,1792]{1,4,3,2,0:T(8,128)(2,1)} %stack.5), calls=%async_computation.4 | async-start | bytes 7340032 | tf_op jit(solution)/shard_map/all_to_all | solution.py:13
  105.7 2.1 copy.46
  107.9 38.6 %all-to-all-done.4 = bf16[4,128,1,2,1792]{1,4,3,2,0:T(8,128)(2,1)} async-done(((bf16[4,128,1,2,1792]{1,4,3,2,0:T(8,128)(2,1)}), bf16[4,128,1,2,1792]{1,4,3,2,0:T(8,128)(2,1)}, u32[]{:S(2)}, u32[]{:S(2)}) %all-to-all-start.4) | async-done | bytes 3670048 | tf_op jit(solution)/shard_map/all_to_all | solution.py:13
  146.4 3.4 %stack.4 = bf16[4,128,1,2,1792]{1,4,3,2,0:T(8,128)(2,1)} broadcast(bf16[128,2,1792]{0,2,1:T(8,128)(2,1)} %copy.46), dimensions={1,3,4} | broadcast | bytes 4587520 | tf_op jit(solution)/shard_map/stack | solution.py:12
  149.9 4.9 %all-to-all-start.2 = ((bf16[4,128,1,2,1792]{1,4,3,2,0:T(8,128)(2,1)}), bf16[4,128,1,2,1792]{1,4,3,2,0:T(8,128)(2,1)}, u32[]{:S(2)}, u32[]{:S(2)}) async-start(bf16[4,128,1,2,1792]{1,4,3,2,0:T(8,128)(2,1)} %stack.4), calls=%async_computation.2 | async-start | bytes 7340032 | tf_op jit(solution)/shard_map/all_to_all | solution.py:13
  154.8 6.4 %fusion.4 = bf16[256,3584]{1,0:T(8,128)(2,1)} fusion(bf16[1,1024,3584]{2,1,0:T(8,128)(2,1)} %all-gather.2.cloned.1.call-done, bf16[1,1,256,1024]{3,2,1,0:T(8,128)(2,1)S(1)} %copy-done.1), kind=kOutput, calls=%fused_computation.6 | convolution fusion | flops 1879965696 | bytes 9699328 | tf_op jit(solution)/shard_map/dot_general | solution.py:33
  161.2 4.7 %reshape.114 = bf16[128,2,3584]{2,1,0:T(2,128)(2,1)} reshape(bf16[256,3584]{1,0:T(8,128)(2,1)} %fusion.4) | data formatting | bytes 3670016 | tf_op jit(solution)/shard_map/reshape | solution.py:37
  165.9 28.9 %all-to-all-done.2 = bf16[4,128,1,2,1792]{1,4,3,2,0:T(8,128)(2,1)} async-done(((bf16[4,128,1,2,1792]{1,4,3,2,0:T(8,128)(2,1)}), bf16[4,128,1,2,1792]{1,4,3,2,0:T(8,128)(2,1)}, u32[]{:S(2)}, u32[]{:S(2)}) %all-to-all-start.2) | async-done | bytes 3670048 | tf_op jit(solution)/shard_map/all_to_all | solution.py:13
  194.8 14.3 %all-to-all-start = ((bf16[128,2,3584]{2,1,0:T(2,128)(2,1)}), bf16[128,2,3584]{2,1,0:T(2,128)(2,1)}, u32[]{:S(2)}, u32[]{:S(2)}) async-start(bf16[128,2,3584]{2,1,0:T(2,128)(2,1)} %reshape.114), calls=%async_computation | async-start | bytes 3670016 | tf_op jit(solution)/shard_map/all_to_all | solution.py:36
  212.1 3.2 %fusion.28 = bf16[256,1792]{0,1:T(8,128)(2,1)S(1)} fusion(bf16[4,128,1,2,1792]{1,4,3,2,0:T(8,128)(2,1)} %all-to-all-done.4, bf16[4,128,2,256]{3,0,2,1:T(4,128)(2,1)S(1)} %bitcast.115), kind=kOutput, calls=%fused_computation.18 | convolution fusion | flops 939982848 | bytes 5111808 | tf_op jit(solution)/shard_map/gsch,sgcd->hd/dot_general | solution.py:68
  215.3 3.2 %fusion.25 = bf16[256,1792]{0,1:T(8,128)(2,1)S(1)} fusion(bf16[4,128,1,2,1792]{1,4,3,2,0:T(8,128)(2,1)} %all-to-all-done.2, bf16[4,128,2,256]{3,0,2,1:T(4,128)(2,1)S(1)} %bitcast.116), kind=kOutput, calls=%fused_computation.17 | convolution fusion | flops 939982848 | bytes 5111808 | tf_op jit(solution)/shard_map/gsch,sgcd->hd/dot_general | solution.py:68
  218.6 2.6 copy.54
  221.2 6.5 %fusion.35 = bf16[1,1,256,1024]{3,2,1,0:T(8,128)(2,1)} fusion(bf16[256,3584]{1,0:T(8,128)(2,1)} %reshape_squeeze.6, bf16[1,1024,3584]{2,1,0:T(8,128)(2,1)} %all-gather.2.cloned.1.call-done), kind=kOutput, calls=%fused_computation.23 | convolution fusion | flops 1879310336 | bytes 9699328 | tf_op jit(solution)/shard_map/rd,hd->rh/dot_general | solution.py:58
  227.7 27.6 %all-to-all-done = bf16[128,2,3584]{2,1,0:T(2,128)(2,1)} async-done(((bf16[128,2,3584]{2,1,0:T(2,128)(2,1)}), bf16[128,2,3584]{2,1,0:T(2,128)(2,1)}, u32[]{:S(2)}, u32[]{:S(2)}) %all-to-all-start) | async-done | bytes 1835040 | tf_op jit(solution)/shard_map/all_to_all | solution.py:36
  255.2 4.1 %reshape.115 = bf16[256,3584]{1,0:T(8,128)(2,1)S(1)} reshape(bf16[128,2,3584]{2,1,0:T(2,128)(2,1)} %all-to-all-done) | data formatting | bytes 3670016 | tf_op jit(solution)/shard_map/reshape | solution.py:39
  (46 shorter events, 12.2 us)
Async XLA Ops:
  7.2 0.8 copy-start.3
  7.2 1.0 copy-start.4
  7.2 1.7 copy-start.2
  7.2 147.6 %all-gather.2.cloned.1.call-start = ((), (), s32[]{:S(2)}) async-start(), calls=%async_computation.5 | async-start | bytes 9175040 | tf_op jit(solution)/shard_map/all_gather | solution.py:32
  13.1 18.6 %copy-start = (bf16[1,1,256,1024]{3,2,1,0:T(8,128)(2,1)S(1)}, bf16[1,1,256,1024]{3,2,1,0:T(8,128)(2,1)}, u32[]{:S(2)}) copy-start(bf16[1,1,256,1024]{3,2,1,0:T(8,128)(2,1)} %param.5) | copy-start | bytes 1572868
  13.1 65.0 %all-to-all-start.1 = ((bf16[128,1,2,3584]{3,2,1,0:T(2,128)(2,1)}), bf16[128,1,2,3584]{3,2,1,0:T(2,128)(2,1)S(1)}, u32[]{:S(2)}, u32[]{:S(2)}) async-start(bf16[128,1,2,3584]{3,2,1,0:T(2,128)(2,1)} %bitcast.111), calls=%async_computation.1 | async-start | bytes 3670016 | tf_op jit(solution)/shard_map/all_to_all | solution.py:50
  78.1 19.1 %all-to-all-start.3 = ((bf16[4,2,32768]{2,1,0:T(2,128)(2,1)}), bf16[4,2,32768]{2,1,0:T(2,128)(2,1)S(1)}, u32[]{:S(2)}, u32[]{:S(2)}) async-start(bf16[4,2,32768]{2,1,0:T(2,128)(2,1)} %reshape.148), calls=%async_computation.3 | async-start | bytes 1048576 | tf_op jit(solution)/shard_map/all_to_all | solution.py:61
  100.8 45.6 %all-to-all-start.4 = ((bf16[4,128,1,2,1792]{1,4,3,2,0:T(8,128)(2,1)}), bf16[4,128,1,2,1792]{1,4,3,2,0:T(8,128)(2,1)}, u32[]{:S(2)}, u32[]{:S(2)}) async-start(bf16[4,128,1,2,1792]{1,4,3,2,0:T(8,128)(2,1)} %stack.5), calls=%async_computation.4 | async-start | bytes 7340032 | tf_op jit(solution)/shard_map/all_to_all | solution.py:13
  149.9 4.9 %copy-start.1 = (bf16[1,1,256,1024]{3,2,1,0:T(8,128)(2,1)S(1)}, bf16[1,1,256,1024]{3,2,1,0:T(8,128)(2,1)}, u32[]{:S(2)}) copy-start(bf16[1,1,256,1024]{3,2,1,0:T(8,128)(2,1)} %param.5) | copy-start | bytes 1572868
  149.9 44.9 %all-to-all-start.2 = ((bf16[4,128,1,2,1792]{1,4,3,2,0:T(8,128)(2,1)}), bf16[4,128,1,2,1792]{1,4,3,2,0:T(8,128)(2,1)}, u32[]{:S(2)}, u32[]{:S(2)}) async-start(bf16[4,128,1,2,1792]{1,4,3,2,0:T(8,128)(2,1)} %stack.4), calls=%async_computation.2 | async-start | bytes 7340032 | tf_op jit(solution)/shard_map/all_to_all | solution.py:13
  194.8 60.4 %all-to-all-start = ((bf16[128,2,3584]{2,1,0:T(2,128)(2,1)}), bf16[128,2,3584]{2,1,0:T(2,128)(2,1)}, u32[]{:S(2)}, u32[]{:S(2)}) async-start(bf16[128,2,3584]{2,1,0:T(2,128)(2,1)} %reshape.114), calls=%async_computation | async-start | bytes 3670016 | tf_op jit(solution)/shard_map/all_to_all | solution.py:36
Sparse Core Ops, SparseCore 0:
  10.1 90.5 all-gather.1
